TPU v7x, 32 devices: a whole 2x2x4 slice. The times are simulated.
32 devices in a mesh: group: 2 (over core), dp: 4 (over z), section: 2 (over x), tensor: 2 (over y).
Axes of the slice: x: 2, y: 2, z: 4, core: 2. Of those that a mesh axis runs over, the one named last changes fastest.
Arguments:
- merged: bfloat16 [768, 5120], P('dp'), may hold values from -6 to 6
- counts: int32 [8], P('dp'), may hold values from 4 to 384
- owners: int32 [768, 1], P('dp'), may hold values from 0 to 3; in each aligned block of 192 rows (0 to 191, 192 to 383, ...) at most 96 rows name the same one
- w_merge: bfloat16 [5120, 8192], P(None, ('group', 'section', 'tensor')), may hold values from -0.078125 to 0.078125
- norm_gain: float32 [8192], P(('group', 'section', 'tensor')), may hold values from 0.25 to 1.75
- cotangent: bfloat16 [4, 4, 96, 8192], P('dp', None, None, ('group', 'section', 'tensor')), may hold values from -6 to 6
Outputs:
- embedded: bfloat16 [4, 4, 96, 8192], P('dp', None, None, ('group', 'section', 'tensor'))
- grad_merged: float32 [768, 5120], P('dp', ('group', 'section', 'tensor'))
- grad_weight: float32 [5120, 8192], P('dp', ('group', 'section', 'tensor'))
Inputs may be any that keep to these rules, and one draw needn't show every extreme that they name: `owners`: in each replica's 192 rows no owner appears more than 96 times.
All inputs are finite; a program needn't handle non-finite values.
Results may differ from a plain program's by a relative error of at most 0.0049.
Values may be sent and summed in bfloat16 or wider, within the bound.
A program may use at most 64 MiB of HBM per device.

v0:
```python
import jax
import jax.numpy as jnp
from jax import lax
from jax.sharding import PartitionSpec as P

D = 8192


def on_device(merged, counts, owners, w_merge, norm_gain, cotangent):
    rows = merged.shape[0]
    columns = w_merge.shape[1]
    replicas = lax.axis_size("dp")
    slots = cotangent.shape[2]
    images = counts.shape[0]
    per_image = rows // images
    projected = jnp.dot(merged, w_merge, preferred_element_type=jnp.float32).astype(jnp.bfloat16)
    row_index = jnp.arange(rows, dtype=jnp.int32)
    image_of = row_index // per_image
    picked = image_of[:, None] == jnp.arange(images, dtype=jnp.int32)[None, :]
    count_of = jnp.sum(jnp.where(picked, counts[None, :], 0), axis=1)
    valid = (4 * (row_index % per_image) < count_of).astype(jnp.float32)
    masked = (projected.astype(jnp.float32) * valid[:, None]).astype(jnp.bfloat16)
    owner = owners[:, 0]
    hits = (owner[:, None] == jnp.arange(replicas, dtype=jnp.int32)[None, :]).astype(jnp.int32)
    before = jnp.cumsum(hits, axis=0) - hits
    slot_index = jnp.sum(before * hits, axis=1)
    target = owner * slots + slot_index
    placer = (jnp.arange(replicas * slots, dtype=jnp.int32)[:, None] == target[None, :]).astype(
        jnp.bfloat16
    )
    outgoing = jnp.dot(placer, masked, preferred_element_type=jnp.float32).astype(jnp.bfloat16)
    outgoing = outgoing.reshape(replicas, slots, columns)
    received = lax.all_to_all(outgoing, "dp", split_axis=0, concat_axis=0, tiled=True)
    values = received.astype(jnp.float32)
    square_sums = lax.psum(jnp.sum(values * values, axis=2), ("group", "section", "tensor"))
    scale = lax.rsqrt(square_sums / D + 1e-05)
    normed = (values * scale[:, :, None] * norm_gain[None, None, :]).astype(jnp.bfloat16)
    embedded = normed[None]
    grad_in = cotangent[0].astype(jnp.float32) * norm_gain[None, None, :]
    inner_sums = lax.psum(jnp.sum(grad_in * values, axis=2), ("group", "section", "tensor"))
    inner = inner_sums / D
    slot_grad = (scale[:, :, None] * grad_in - values * (scale**3 * inner)[:, :, None]).astype(
        jnp.bfloat16
    )
    returned = lax.all_to_all(slot_grad, "dp", split_axis=0, concat_axis=0, tiled=True)
    returned = returned.reshape(replicas * slots, columns)
    gathered = lax.dot_general(
        placer, returned, (((0,), (0,)), ((), ())), preferred_element_type=jnp.float32
    )
    back = (gathered * valid[:, None]).astype(jnp.bfloat16)
    input_terms = lax.dot_general(
        back, w_merge, (((1,), (1,)), ((), ())), preferred_element_type=jnp.float32
    )
    grad_merged = lax.psum_scatter(
        input_terms, ("group", "section", "tensor"), scatter_dimension=1, tiled=True
    )
    column_block = lax.all_to_all(merged, "dp", split_axis=1, concat_axis=0, tiled=True)
    grad_weight = lax.dot_general(
        column_block,
        lax.all_gather(back, "dp", axis=0, tiled=True),
        (((0,), (0,)), ((), ())),
        preferred_element_type=jnp.float32,
    )
    return (embedded, grad_merged, grad_weight)


def solution(mesh):
    placed = (
        P("dp", None),
        P("dp"),
        P("dp", None),
        P(None, ("group", "section", "tensor")),
        P(("group", "section", "tensor")),
        P("dp", None, None, ("group", "section", "tensor")),
    )
    return jax.shard_map(
        on_device,
        mesh=mesh,
        in_specs=placed,
        out_specs=(
            P("dp", None, None, ("group", "section", "tensor")),
            P("dp", ("group", "section", "tensor")),
            P("dp", ("group", "section", "tensor")),
        ),
        check_vma=False,
    )
```

profile of v0, /device:TPU:0, one launch (start us, length us, event | category | flops | bytes accessed | tf_op | source)
XLA Modules:
  0.0 182.4 jit_solution(6930971145670902794)
XLA Ops:
  8.0 0.0 all-gather.2.cloned.1.call-start
  8.1 0.7 iota_compare_fusion.3
  8.7 0.7 fusion.18
  9.5 1.2 reduce-window.6
  10.8 0.1 slice.12
  10.8 0.1 copy.23
  11.0 0.1 copy.24
  11.1 0.1 add_bitcast_fusion
  11.2 0.7 fusion.16
  11.9 0.7 multiply_add_fusion
  12.5 0.0 copy-start.2
  12.5 7.0 %convolution_convert_fusion = bf16[384,1024]{1,0:T(8,128)(2,1)S(1)} fusion(bf16[192,5120]{1,0:T(8,128)(2,1)} %param.6, bf16[5120,1024]{1,0:T(8,128)(2,1)} %param.9, f32[192]{0:T(256)S(1)} %compare_convert_fusion, s32[192]{0:T(256)S(1)} %multiply_add_fusion), kind=kOutput, calls=%fused_computation.14 | convolution fusion | flops 2165514240 | bytes 13239808 | tf_op jit(solution)/shard_map/dot_general | solution.py:31
  19.6 0.0 copy-start
  19.6 26.4 %all_to_all.29 = bf16[4,96,1024]{2,1,0:T(8,128)(2,1)S(1)} all-to-all(bf16[4,96,1024]{2,1,0:T(8,128)(2,1)S(1)} %bitcast.38), channel_id=1, replica_groups=mesh['group'=2,'dp'=4,'section'=2,'tensor'=2] {'dp'}, dimensions={0} | all-to-all | bytes 1572864 | tf_op jit(solution)/shard_map/all_to_all | solution.py:33
  46.0 0.0 copy-done.2
  46.0 0.0 copy-done
  46.0 0.4 fusion.3
  46.4 14.3 %all-reduce.1 = (f32[4,96]{1,0:T(4,128)S(1)}, f32[4,96]{1,0:T(4,128)S(1)}) all-reduce(f32[4,96]{1,0:T(4,128)S(1)} %get-tuple-element.19, f32[4,96]{1,0:T(4,128)S(1)} %get-tuple-element.18), channel_id=1, replica_groups=mesh['group'=2,'dp'=4,'section'=2,'tensor'=2] {'group','section','tensor'}, use_global_device_ids=true, to_apply=%region_5.6 | all-reduce | flops 768 | bytes 6144 | tf_op jit(solution)/shard_map/psum | solution.py:35
  60.7 1.4 fusion.5
  62.1 23.6 %all_to_all.30 = bf16[4,96,1024]{2,1,0:T(8,128)(2,1)S(1)} all-to-all(bf16[4,96,1024]{2,1,0:T(8,128)(2,1)S(1)} %get-tuple-element.22), channel_id=1, replica_groups=mesh['group'=2,'dp'=4,'section'=2,'tensor'=2] {'dp'}, dimensions={0} | all-to-all | bytes 1572864 | tf_op jit(solution)/shard_map/all_to_all | solution.py:45
  85.7 1.2 fusion.7
  86.9 0.0 all-gather.2.cloned.1.call-update
  86.9 0.0 reduce-scatter.2.cloned.1.call-start
  86.9 9.7 %fusion.21 = f32[192,5120]{1,0:T(8,128)} fusion(bf16[192,1024]{1,0:T(8,128)(2,1)} %fusion.7, bf16[5120,1024]{1,0:T(8,128)(2,1)} %param.9), kind=kOutput, calls=%fused_computation.48 | convolution fusion | flops 2013265920 | bytes 14811136 | tf_op jit(solution)/shard_map/dot_general | solution.py:51
  96.7 0.0 copy-start.1
  96.7 0.0 reduce-scatter.2.cloned.1.call-update
  96.7 1.5 copy-done.1
  98.2 0.1 copy.31
  98.3 64.7 %all_to_all.31 = bf16[192,4,1280]{2,0,1:T(8,128)(2,1)S(1)} all-to-all(bf16[192,4,1280]{2,0,1:T(8,128)(2,1)S(1)} %bitcast.34), channel_id=1, replica_groups=mesh['group'=2,'dp'=4,'section'=2,'tensor'=2] {'dp'}, dimensions={1} | all-to-all | bytes 3932160 | tf_op jit(solution)/shard_map/all_to_all | solution.py:57
  163.1 0.0 all-gather.2.cloned.1.call-done
  163.1 6.0 %convolution_bitcast_fusion = f32[1280,1024]{0,1:T(8,128)} fusion(bf16[768,1024]{1,0:T(8,128)(2,1)} %all-gather.2.cloned.1.call-done, bf16[768,1280]{1,0:T(8,128)(2,1)S(1)} %bitcast.37), kind=kOutput, calls=%fused_computation | convolution fusion | flops 2013265920 | bytes 8781824 | tf_op jit(solution)/shard_map/dot_general | solution.py:58
  169.1 5.9 %copy.26 = f32[1280,1024]{1,0:T(8,128)} copy(f32[1280,1024]{0,1:T(8,128)} %convolution_bitcast_fusion) | data formatting | bytes 10485760
  174.9 0.0 reduce-scatter.2.cloned.1.call-done
  (8 shorter events, 0.1 us)
Async XLA Ops:
  8.0 155.1 %all-gather.2.cloned.1.call-start = ((), (), s32[]{:S(2)}) async-start(), calls=%async_computation.5 | async-start | bytes 1966080 | tf_op jit(solution)/shard_map/all_gather | solution.py:60
  12.5 33.4 %copy-start.2 = (f32[1024]{0:T(1024)S(1)}, f32[1024]{0:T(1024)}, u32[]{:S(2)}) copy-start(f32[1024]{0:T(1024)} %param.10) | copy-start | bytes 12292
  19.6 26.4 %copy-start = (bf16[1,4,96,1024]{3,2,1,0:T(8,128)(2,1)S(1)}, bf16[1,4,96,1024]{3,2,1,0:T(8,128)(2,1)}, u32[]{:S(2)}) copy-start(bf16[1,4,96,1024]{3,2,1,0:T(8,128)(2,1)} %param.11) | copy-start | bytes 2359300
  86.9 88.1 %reduce-scatter.2.cloned.1.call-start = ((), (), s32[]{:S(2)}) async-start(), calls=%async_computation.4 | async-start | bytes 4423680 | tf_op jit(solution)/shard_map/reduce_scatter | solution.py:54
  96.7 1.5 copy-start.1
Sparse Core Ops, SparseCore 0:
  87.0 58.4 all-gather.1
Sparse Core Ops, SparseCore 1:
  96.8 46.7 reduce-scatter.1
where the time goes:
time: 183 us; the launch traced here: 182 us
  blocking collectives  129 us (70%)
  matrix products  23.9 us (13%)
  between operations  15.5 us (8%)
  local copies, waits for them, and re-layouts  7.84 us (4%)
  other arithmetic  6.04 us (3%)
    all_to_all x1, blocking collectives, on_device(): lax.all_to_all(merged, 'dp', split_axis=1, concat_axis=0, tiled=True)  64.7 us
    all_to_all x1, blocking collectives, on_device(): lax.all_to_all(outgoing, 'dp', split_axis=0, concat_axis=0, tiled=True)  26.4 us
    all_to_all x1, blocking collectives, on_device(): lax.all_to_all(slot_grad, 'dp', split_axis=0, concat_axis=0, tiled=True)  23.6 us
    psum x1, blocking collectives, on_device(): lax.psum(jnp.sum(values * values, axis=2), ('group', 'section', 'tensor'))  14.3 us
    dot_general x1, matrix products, on_device(): lax.dot_general(back, w_merge, (((1,), (1,)), ((), ())), preferred_elemen...  9.72 us
    unnamed x8, local copies, waits for them, and re-layouts  7.42 us
    dot_general x1, matrix products, on_device(): jnp.dot(placer, masked, preferred_element_type=jnp.float32)  7.02 us
    dot_general x1, matrix products, on_device(): lax.dot_general(column_block, lax.all_gather(back, 'dp', axis=0, tiled=Tr...  5.97 us
  transfers between devices with their start and end apart: 2, of which 0 were waited for; matrix products, arithmetic and copies ran while one was open for 12% of the time, Pallas kernels for 0%

commit v1 on v0

--- a/solution.py
+++ b/solution.py
@@ -54,7 +54,10 @@
     grad_merged = lax.psum_scatter(
         input_terms, ("group", "section", "tensor"), scatter_dimension=1, tiled=True
     )
-    column_block = lax.all_to_all(merged, "dp", split_axis=1, concat_axis=0, tiled=True)
+    column_block = jnp.concatenate(
+        lax.all_to_all(jnp.stack(jnp.split(merged, lax.axis_size("dp"), axis=1)), "dp", 0, 0),
+        axis=0,
+    )
     grad_weight = lax.dot_general(
         column_block,
         lax.all_gather(back, "dp", axis=0, tiled=True),

time: 183 us -> 177 us (0.967)
  local copies, waits for them, and re-layouts: 7.84 us -> 1.96 us
    unnamed x8 -> x7, local copies, waits for them, and re-layouts: 7.42 us -> 1.54 us
  transfers between devices with their start and end apart: 2 -> 2, of which waited for: 0 -> 0; matrix products, arithmetic and copies ran while one was open for 12% -> 9% of each run, Pallas kernels for 0% -> 0%
where the time goes in v1:
time: 177 us
  blocking collectives  129 us (73%)
  matrix products  23.8 us (13%)
  between operations  15.5 us (9%)
  other arithmetic  6.29 us (4%)
  local copies, waits for them, and re-layouts  1.96 us (1%)
    all_to_all x1, blocking collectives, on_device(): lax.all_to_all(jnp.stack(jnp.split(merged, lax.axis_size('dp'), axis=1)),...  64.6 us
    all_to_all x1, blocking collectives, on_device(): lax.all_to_all(outgoing, 'dp', split_axis=0, concat_axis=0, tiled=True)  26.4 us
    all_to_all x1, blocking collectives, on_device(): lax.all_to_all(slot_grad, 'dp', split_axis=0, concat_axis=0, tiled=True)  23.6 us
    psum x1, blocking collectives, on_device(): lax.psum(jnp.sum(values * values, axis=2), ('group', 'section', 'tensor'))  14.3 us
    dot_general x1, matrix products, on_device(): lax.dot_general(back, w_merge, (((1,), (1,)), ((), ())), preferred_elemen...  9.65 us
    dot_general x1, matrix products, on_device(): jnp.dot(placer, masked, preferred_element_type=jnp.float32)  7.02 us
    dot_general x1, matrix products, on_device(): lax.dot_general(column_block, lax.all_gather(back, 'dp', axis=0, tiled=Tr...  6.01 us
  transfers between devices with their start and end apart: 2, of which 0 were waited for; matrix products, arithmetic and copies ran while one was open for 9% of the time, Pallas kernels for 0%

profile of v1, /device:TPU:0, one launch (start us, length us, event | category | flops | bytes accessed | tf_op | source)
XLA Modules:
  0.0 176.5 jit_solution(17498395571306647157)
XLA Ops:
  8.0 0.0 all-gather.2.cloned.1.call-start
  8.1 0.7 fusion.18
  8.8 0.7 iota_compare_fusion.3
  9.5 1.2 reduce-window.6
  10.7 0.1 slice.12
  10.8 0.1 copy.11
  11.0 0.1 copy.12
  11.1 0.1 add_bitcast_fusion
  11.1 0.7 fusion.16
  11.8 0.7 multiply_add_fusion
  12.5 0.0 copy-start.2
  12.5 7.0 %convolution_convert_fusion = bf16[384,1024]{1,0:T(8,128)(2,1)S(1)} fusion(bf16[192,5120]{1,0:T(8,128)(2,1)} %param.6, bf16[5120,1024]{1,0:T(8,128)(2,1)} %param.9, f32[192]{0:T(256)S(1)} %compare_convert_fusion, s32[192]{0:T(256)S(1)} %multiply_add_fusion), kind=kOutput, calls=%fused_computation.13 | convolution fusion | flops 2165514240 | bytes 13239808 | tf_op jit(solution)/shard_map/dot_general | solution.py:31
  19.6 0.0 copy-start
  19.6 26.4 %all_to_all.15 = bf16[4,96,1024]{2,1,0:T(8,128)(2,1)S(1)} all-to-all(bf16[4,96,1024]{2,1,0:T(8,128)(2,1)S(1)} %bitcast.36), channel_id=1, replica_groups=mesh['group'=2,'dp'=4,'section'=2,'tensor'=2] {'dp'}, dimensions={0} | all-to-all | bytes 1572864 | tf_op jit(solution)/shard_map/all_to_all | solution.py:33
  46.0 0.0 copy-done.2
  46.0 0.0 copy-done
  46.0 0.4 fusion.3
  46.4 14.3 %all-reduce.1 = (f32[4,96]{1,0:T(4,128)S(1)}, f32[4,96]{1,0:T(4,128)S(1)}) all-reduce(f32[4,96]{1,0:T(4,128)S(1)} %get-tuple-element.4, f32[4,96]{1,0:T(4,128)S(1)} %get-tuple-element.3), channel_id=1, replica_groups=mesh['group'=2,'dp'=4,'section'=2,'tensor'=2] {'group','section','tensor'}, use_global_device_ids=true, to_apply=%region_5.6 | all-reduce | flops 768 | bytes 6144 | tf_op jit(solution)/shard_map/psum | solution.py:35
  60.7 1.4 fusion.5
  62.1 23.6 %all_to_all.16 = bf16[4,96,1024]{2,1,0:T(8,128)(2,1)S(1)} all-to-all(bf16[4,96,1024]{2,1,0:T(8,128)(2,1)S(1)} %get-tuple-element.11), channel_id=1, replica_groups=mesh['group'=2,'dp'=4,'section'=2,'tensor'=2] {'dp'}, dimensions={0} | all-to-all | bytes 1572864 | tf_op jit(solution)/shard_map/all_to_all | solution.py:45
  85.7 1.2 fusion.7
  86.9 0.0 all-gather.2.cloned.1.call-update
  86.9 0.0 reduce-scatter.2.cloned.1.call-start
  86.9 9.7 %fusion.21 = f32[192,5120]{1,0:T(8,128)} fusion(bf16[192,1024]{1,0:T(8,128)(2,1)} %fusion.7, bf16[5120,1024]{1,0:T(8,128)(2,1)} %param.9), kind=kOutput, calls=%fused_computation.51 | convolution fusion | flops 2013265920 | bytes 14811136 | tf_op jit(solution)/shard_map/dot_general | solution.py:51
  96.6 0.0 copy-start.1
  96.6 0.0 reduce-scatter.2.cloned.1.call-update
  96.6 1.5 copy-done.1
  98.1 0.1 slice_bitcast_fusion.3
  98.3 0.2 pad_maximum_fusion
  98.5 64.6 %all_to_all.17 = bf16[4,192,1280]{2,1,0:T(8,128)(2,1)S(1)} all-to-all(bf16[4,192,1280]{2,1,0:T(8,128)(2,1)S(1)} %pad_maximum_fusion), channel_id=1, replica_groups=mesh['group'=2,'dp'=4,'section'=2,'tensor'=2] {'dp'}, dimensions={0} | all-to-all | bytes 3932160 | tf_op jit(solution)/shard_map/all_to_all | solution.py:58
  163.1 0.0 all-gather.2.cloned.1.call-done
  163.1 6.0 %fusion.22 = f32[1280,1024]{1,0:T(8,128)} fusion(bf16[768,1280]{1,0:T(8,128)(2,1)S(1)} %bitcast.35, bf16[768,1024]{1,0:T(8,128)(2,1)} %all-gather.2.cloned.1.call-done), kind=kOutput, calls=%fused_computation.52 | convolution fusion | flops 2013265920 | bytes 8781824 | tf_op jit(solution)/shard_map/dot_general | solution.py:61
  169.1 0.0 reduce-scatter.2.cloned.1.call-done
  (8 shorter events, 0.1 us)
Async XLA Ops:
  8.0 155.1 %all-gather.2.cloned.1.call-start = ((), (), s32[]{:S(2)}) async-start(), calls=%async_computation.5 | async-start | bytes 1966080 | tf_op jit(solution)/shard_map/all_gather | solution.py:63
  12.5 33.4 %copy-start.2 = (f32[1024]{0:T(1024)S(1)}, f32[1024]{0:T(1024)}, u32[]{:S(2)}) copy-start(f32[1024]{0:T(1024)} %param.10) | copy-start | bytes 12292
  19.6 26.4 %copy-start = (bf16[1,4,96,1024]{3,2,1,0:T(8,128)(2,1)S(1)}, bf16[1,4,96,1024]{3,2,1,0:T(8,128)(2,1)}, u32[]{:S(2)}) copy-start(bf16[1,4,96,1024]{3,2,1,0:T(8,128)(2,1)} %param.11) | copy-start | bytes 2359300
  86.9 82.2 %reduce-scatter.2.cloned.1.call-start = ((), (), s32[]{:S(2)}) async-start(), calls=%async_computation.4 | async-start | bytes 4423680 | tf_op jit(solution)/shard_map/reduce_scatter | solution.py:54
  96.6 1.5 copy-start.1
Sparse Core Ops, SparseCore 0:
  87.0 58.3 all-gather.1
Sparse Core Ops, SparseCore 1:
  96.7 46.7 reduce-scatter.1
